TPU v7x, 32 devices: a whole 2x2x4 slice. The times are simulated.
32 devices in a mesh: space: 4 (over y, x), orb: 8 (over z, core).
Axes of the slice: x: 2, y: 2, z: 4, core: 2. Of those that a mesh axis runs over, the one named last changes fastest.
Arguments:
- orbitals: float32 [16, 16, 32, 1024], P('space', None, None, 'orb'), may hold values from -6 to 6
- potential: float32 [16, 16, 32], P('space'), may hold values from 0 to 2
Outputs:
- updated: float32 [16, 16, 32, 1024], P('space', None, None, 'orb')
All inputs are finite; a program needn't handle non-finite values.
Results may differ from a plain program's by a relative error of at most 0.00007.
Values sent between devices are 32-bit elements; how exact they have to be, the bound alone decides.
A program may use at most 64 MiB of HBM per device.

v0:
```python
import jax
import jax.numpy as jnp
from jax import lax
from jax.sharding import PartitionSpec as P

PANEL = 512
DEGREE = 4
STENCIL = (-205.0 / 72.0, 8.0 / 5.0, -1.0 / 5.0, 8.0 / 315.0, -1.0 / 560.0)
SHIFT_MID = 7.25
HALF_WIDTH = 4.75


def padded_2(shard, sides, width):
    for axis, dim in sides:
        count, length = (lax.axis_size(axis), shard.shape[dim])
        up = [(i, (i + 1) % count) for i in range(count)]
        down = [(j, i) for i, j in up]
        last = lax.slice_in_dim(shard, length - width, length, axis=dim)
        leading = lax.slice_in_dim(shard, 0, width, axis=dim)
        before = lax.ppermute(last, axis, up)
        after = lax.ppermute(leading, axis, down)
        shard = jnp.concatenate([before, shard, after], axis=dim)
    return shard


def hamilton(field, potential):
    planes = field.shape[0]
    padded = padded_2(field, (("space", 0),), 4)
    laplace = 3.0 * STENCIL[0] * field
    for offset in range(1, 5):
        upper = padded[4 + offset : 4 + offset + planes]
        below = padded[4 - offset : 4 - offset + planes]
        laplace = laplace + STENCIL[offset] * (upper + below)
    for axis in (1, 2):
        for offset in range(1, 5):
            laplace = laplace + STENCIL[offset] * (
                jnp.roll(field, offset, axis) + jnp.roll(field, -offset, axis)
            )
    return -0.5 * laplace + potential[..., None] * field


def chebyshev(block, potential):
    before = block
    current = (hamilton(block, potential) - SHIFT_MID * block) / HALF_WIDTH
    for order in range(DEGREE - 1):
        following = 2.0 * (hamilton(current, potential) - SHIFT_MID * current) / HALF_WIDTH - before
        before, current = (current, following)
    return current


def per_device(orbitals, potential):
    highest = lax.Precision.HIGHEST
    filtered = chebyshev(orbitals, potential)
    planes, rows_y, rows_z, columns = filtered.shape
    local_points = planes * rows_y * rows_z
    points = local_points * lax.axis_size("space")
    panel_dev = PANEL // lax.axis_size("orb")
    flat = filtered.reshape(local_points, columns)
    panel_own = flat[:, :panel_dev]
    trailing = flat[:, panel_dev:]
    panel = lax.all_gather(panel_own, "orb", axis=1, tiled=True)
    coupling_part = jnp.dot(panel.T, trailing, precision=highest)
    gram_part = jnp.dot(panel.T, panel, precision=highest)
    gram_full, coupling = lax.psum((gram_part, coupling_part), "space")
    gram_full = gram_full / points
    coupling = coupling / points
    lower_factor = jnp.linalg.cholesky(gram_full)
    identity = jnp.eye(PANEL, dtype=jnp.float32)
    inverse = lax.linalg.triangular_solve(lower_factor, identity, left_side=True, lower=True)
    start = lax.axis_index("orb") * panel_dev
    own_rows = lax.dynamic_slice_in_dim(inverse, start, panel_dev, 0)
    ortho_own = jnp.dot(panel, own_rows.T, precision=highest)
    middle = jnp.dot(inverse, coupling, precision=highest)
    project = jnp.dot(inverse.T, middle, precision=highest)
    trailing_new = trailing - jnp.dot(panel, project, precision=highest)
    joined = jnp.concatenate([ortho_own, trailing_new], axis=1)
    return joined.reshape(planes, rows_y, rows_z, columns)


def solution(mesh):
    placed = (P("space", None, None, "orb"), P("space", None, None))
    return jax.shard_map(
        per_device,
        mesh=mesh,
        in_specs=placed,
        out_specs=P("space", None, None, "orb"),
        check_vma=False,
    )
```

profile of v0, /device:TPU:0, one launch (start us, length us, event | category | flops | bytes accessed | tf_op | source)
XLA Modules:
  0.0 514.7 jit_solution(1693416008679827727)
XLA Ops:
  6.5 3.0 collective-permute-start.1
  10.5 1.9 fusion.217
  12.9 1.1 fusion.211
  14.0 1.1 fusion.213
  15.0 1.4 fusion.215
  21.2 13.6 %collective-permute-done.1 = f32[4,16,32,128]{3,2,1,0:T(8,128)S(1)} collective-permute-done((f32[4,16,32,128]{3,2,1,0:T(8,128)}, f32[4,16,32,128]{3,2,1,0:T(8,128)S(1)}, u32[]{:S(2)}, u32[]{:S(2)}) %collective-permute-start.1) | collective-permute-done | bytes 1048608 | tf_op jit(solution)/shard_map/ppermute | solution.py:20
  35.0 21.6 %collective-permute-done = f32[4,16,32,128]{3,2,1,0:T(8,128)S(1)} collective-permute-done((f32[4,16,32,128]{3,2,1,0:T(8,128)}, f32[4,16,32,128]{3,2,1,0:T(8,128)S(1)}, u32[]{:S(2)}, u32[]{:S(2)}) %collective-permute-start) | collective-permute-done | bytes 1048608 | tf_op jit(solution)/shard_map/ppermute | solution.py:21
  56.6 5.3 %broadcast_multiply_fusion.1 = (f32[4,16,32,128]{3,2,1,0:T(8,128)S(1)}, f32[4,16,32,128]{3,2,1,0:T(8,128)S(1)}) fusion(f32[4,16,32,128]{3,2,1,0:T(8,128)S(1)} %copy-done, f32[4,16,32]{2,1,0:T(8,128)S(1)} %copy-done.12, f32[4,16,4,128]{3,2,1,0:T(4,128)} %get-tuple-element.156, f32[4,16,28,128]{3,2,1,0:T(8,128)S(1)} %get-tuple-element.158, ...), kind=kLoop, calls=%fused_computation.211 | loop fusion | flops 15466496 | bytes 28319744 | tf_op jit(solution)/shard_map/div | solution.py:44
  63.8 1.3 fusion.199
  69.5 1.4 collective-permute-start.2
  72.9 22.7 %collective-permute-done.2 = f32[4,16,32,128]{3,2,1,0:T(8,128)S(1)} collective-permute-done((f32[4,16,32,128]{3,2,1,0:T(8,128)S(1)}, f32[4,16,32,128]{3,2,1,0:T(8,128)S(1)}, u32[]{:S(2)}, u32[]{:S(2)}) %collective-permute-start.2) | collective-permute-done | bytes 1048608 | tf_op jit(solution)/shard_map/ppermute | solution.py:21
  95.6 20.6 %collective-permute-done.3 = f32[4,16,32,128]{3,2,1,0:T(8,128)S(1)} collective-permute-done((f32[4,16,32,128]{3,2,1,0:T(8,128)S(1)}, f32[4,16,32,128]{3,2,1,0:T(8,128)S(1)}, u32[]{:S(2)}, u32[]{:S(2)}) %collective-permute-start.3) | collective-permute-done | bytes 1048608 | tf_op jit(solution)/shard_map/ppermute | solution.py:20
  117.2 6.9 %multiply_subtract_fusion.2 = f32[4,16,32,128]{3,2,1,0:T(8,128)S(1)} fusion(f32[4,16,32,128]{3,2,1,0:T(8,128)S(1)} %copy-done, f32[4,16,32,128]{3,2,1,0:T(8,128)S(1)} %get-tuple-element.24, f32[4,16,4,128]{3,2,1,0:T(4,128)} %get-tuple-element.122, f32[4,16,28,128]{3,2,1,0:T(8,128)S(1)} %get-tuple-element.124, f32[4,16,28,128]{3,2,1,0:T(8,128)S(1)} %get-tuple-element.123, ...), kind=kLoop, calls=%fused_computation.201 | loop fusion | flops 17301504 | bytes 23076864 | tf_op jit(solution)/shard_map/sub | solution.py:46
  126.0 2.3 collective-permute-start.4
  135.1 17.0 %collective-permute-done.4 = f32[4,16,32,128]{3,2,1,0:T(8,128)S(1)} collective-permute-done((f32[4,16,32,128]{3,2,1,0:T(8,128)S(1)}, f32[4,16,32,128]{3,2,1,0:T(8,128)S(1)}, u32[]{:S(2)}, u32[]{:S(2)}) %collective-permute-start.4) | collective-permute-done | bytes 1048608 | tf_op jit(solution)/shard_map/ppermute | solution.py:21
  152.1 20.4 %collective-permute-done.5 = f32[4,16,32,128]{3,2,1,0:T(8,128)S(1)} collective-permute-done((f32[4,16,32,128]{3,2,1,0:T(8,128)S(1)}, f32[4,16,32,128]{3,2,1,0:T(8,128)S(1)}, u32[]{:S(2)}, u32[]{:S(2)}) %collective-permute-start.5) | collective-permute-done | bytes 1048608 | tf_op jit(solution)/shard_map/ppermute | solution.py:20
  173.5 6.9 %multiply_subtract_fusion.1 = f32[4,16,32,128]{3,2,1,0:T(8,128)S(1)} fusion(f32[4,16,32,128]{3,2,1,0:T(8,128)S(1)} %multiply_subtract_fusion.2, f32[4,16,4,128]{3,2,1,0:T(4,128)} %get-tuple-element.90, f32[4,16,28,128]{3,2,1,0:T(8,128)S(1)} %get-tuple-element.92, f32[4,16,28,128]{3,2,1,0:T(8,128)S(1)} %get-tuple-element.91, ...), kind=kLoop, calls=%fused_computation.200 | loop fusion | flops 17563648 | bytes 22028288 | tf_op jit(solution)/shard_map/sub | solution.py:46
  181.3 1.3 fusion.167
  182.6 1.4 collective-permute-start.6
  190.4 18.2 %collective-permute-done.6 = f32[4,16,32,128]{3,2,1,0:T(8,128)S(1)} collective-permute-done((f32[4,16,32,128]{3,2,1,0:T(8,128)S(1)}, f32[4,16,32,128]{3,2,1,0:T(8,128)S(1)}, u32[]{:S(2)}, u32[]{:S(2)}) %collective-permute-start.6) | collective-permute-done | bytes 1048608 | tf_op jit(solution)/shard_map/ppermute | solution.py:21
  208.7 19.4 %collective-permute-done.7 = f32[4,16,32,128]{3,2,1,0:T(8,128)S(1)} collective-permute-done((f32[4,16,32,128]{3,2,1,0:T(8,128)S(1)}, f32[4,16,32,128]{3,2,1,0:T(8,128)S(1)}, u32[]{:S(2)}, u32[]{:S(2)}) %collective-permute-start.7) | collective-permute-done | bytes 1048608 | tf_op jit(solution)/shard_map/ppermute | solution.py:20
  229.1 6.8 %multiply_subtract_fusion = f32[4,16,32,128]{3,2,1,0:T(8,128)S(1)} fusion(f32[4,16,32,128]{3,2,1,0:T(8,128)S(1)} %multiply_subtract_fusion.2, f32[4,16,32,128]{3,2,1,0:T(8,128)S(1)} %multiply_subtract_fusion.1, f32[4,16,4,128]{3,2,1,0:T(4,128)} %get-tuple-element.58, f32[4,16,28,128]{3,2,1,0:T(8,128)S(1)} %get-tuple-element.60, ...), kind=kLoop, calls=%fused_computation.199 | loop fusion | flops 17301504 | bytes 22028288 | tf_op jit(solution)/shard_map/sub | solution.py:46
  236.3 1.1 copy.11
  237.5 47.5 %all-gather.2.cloned.1.call-done = f32[2048,512]{0,1:T(8,128)} async-done(((f32[2048,64]{0,1:T(8,128)}), f32[2048,512]{0,1:T(8,128)}) %all-gather.2.cloned.1.call-update) | async-done | bytes 4194320 | tf_op jit(solution)/shard_map/all_gather | solution.py:61
  285.0 10.7 %fusion.224 = f32[512,512]{0,1:T(8,128)} fusion(f32[2048,512]{0,1:T(8,128)} %all-gather.2.cloned.1.call-done), kind=kOutput, calls=%fused_computation.337 | convolution fusion | flops 6442450944 | bytes 5242880 | tf_op jit(solution)/shard_map/dot_general | solution.py:63
  295.7 4.9 fusion.154
  300.8 1.1 fusion.125
  301.9 1.1 copy.17
  303.0 51.0 %all-reduce.4.cloned.1.call-done = (f32[512,64]{0,1:T(8,128)}, f32[512,512]{0,1:T(8,128)}) async-done(((f32[512,64]{0,1:T(8,128)}, f32[512,512]{0,1:T(8,128)}), (f32[512,64]{0,1:T(8,128)}, f32[512,512]{0,1:T(8,128)})) %all-reduce.4.cloned.1.call-update) | async-done | bytes 1179664 | tf_op jit(solution)/shard_map/psum | solution.py:64
  354.0 1.4 broadcast_multiply_fusion
  356.0 11.7 %cholesky.104 = f32[128,128]{1,0:T(8,128)S(1)} custom-call(f32[128,128]{1,0:T(8,128)S(1)} %cholesky.266), custom_call_target="Cholesky" | custom-call | tf_op jit(solution)/shard_map/jit(cholesky)/cholesky | solution.py:67
  367.9 9.8 %custom-call.30 = f32[1,128,128]{1,2,0:T(8,128)S(1)} custom-call(f32[1,128,128]{2,1,0:T(8,128)S(1)} %get-tuple-element.168), custom_call_target="InvertDiagBlocksLowerTriangular" | custom-call | tf_op jit(solution)/shard_map/jit(cholesky)/cholesky | solution.py:67
  378.4 11.9 %cholesky.217 = f32[128,128]{1,0:T(8,128)S(1)} custom-call(f32[128,128]{1,0:T(8,128)S(1)} %cholesky.270), custom_call_target="Cholesky" | custom-call | tf_op jit(solution)/shard_map/jit(cholesky)/cholesky | solution.py:67
  390.3 9.8 %custom-call.31 = f32[1,128,128]{1,2,0:T(8,128)S(1)} custom-call(f32[1,128,128]{2,1,0:T(8,128)S(1)} %get-tuple-element.165), custom_call_target="InvertDiagBlocksLowerTriangular" | custom-call | tf_op jit(solution)/shard_map/jit(cholesky)/cholesky | solution.py:67
  400.8 12.3 %cholesky.238 = f32[128,128]{1,0:T(8,128)} custom-call(f32[128,128]{1,0:T(8,128)S(1)} %cholesky.275), custom_call_target="Cholesky" | custom-call | tf_op jit(solution)/shard_map/jit(cholesky)/cholesky | solution.py:67
  413.1 1.6 select_reduce_fusion.1
  415.4 11.3 %custom-call.32 = f32[1,128,128]{1,2,0:T(8,128)} custom-call(f32[1,128,128]{2,1,0:T(8,128)} %get-tuple-element.162), custom_call_target="InvertDiagBlocksLowerTriangular" | custom-call | tf_op jit(solution)/shard_map/jit(cholesky)/cholesky | solution.py:67
  428.1 11.9 %cholesky.255 = f32[128,128]{1,0:T(8,128)S(1)} custom-call(f32[128,128]{1,0:T(8,128)S(1)} %convolution_subtract_fusion.6), custom_call_target="Cholesky" | custom-call | tf_op jit(solution)/shard_map/jit(cholesky)/cholesky | solution.py:67
  444.2 10.8 %while.1 = (s32[]{:T(128)}, f32[512,512]{1,0:T(8,128)S(1)}, s32[4,2]{0,1:T(2,128)S(1)}, f32[4,128,128]{2,1,0:T(8,128)}, s32[]{:T(128)}) while((s32[]{:T(128)}, f32[512,512]{1,0:T(8,128)S(1)}, s32[4,2]{0,1:T(2,128)S(1)}, f32[4,128,128]{2,1,0:T(8,128)}, s32[]{:T(128)}) %tuple.94), condition=%wide.while_cond, body=%wide.while_body.sunk | while | flops 2 | bytes 132705 | solution.py:69
  444.9 2.0 bitcast_dynamic-update-slice_fusion.2
  447.5 2.0 bitcast_dynamic-update-slice_fusion.2
  450.2 2.0 bitcast_dynamic-update-slice_fusion.2
  452.9 2.0 bitcast_dynamic-update-slice_fusion.2
  455.0 40.1 %custom-call.33 = f32[4,128,128]{1,2,0:T(8,128)S(1)} custom-call(f32[4,128,128]{2,1,0:T(8,128)} %get-tuple-element.12), custom_call_target="InvertDiagBlocksLowerTriangular" | custom-call | tf_op jit(solution)/shard_map/triangular_solve | solution.py:69
  498.3 1.1 fusion.136
  500.4 2.8 fusion.138
  503.2 2.8 convolution_subtract_fusion
  506.1 1.3 copy.15
  (142 shorter events, 46.4 us)
Async XLA Ops:
  6.5 5.8 %copy-start = (f32[4,16,32,128]{3,2,1,0:T(8,128)S(1)}, f32[4,16,32,128]{3,2,1,0:T(8,128)}, u32[]{:S(2)}) copy-start(f32[4,16,32,128]{3,2,1,0:T(8,128)} %param.2) | copy-start | bytes 3145732
  6.5 278.4 %all-gather.2.cloned.1.call-start = ((), (), s32[]{:S(2)}) async-start(), calls=%async_computation | async-start | bytes 4718592 | tf_op jit(solution)/shard_map/all_gather | solution.py:61
  6.5 28.2 %collective-permute-start.1 = (f32[4,16,32,128]{3,2,1,0:T(8,128)}, f32[4,16,32,128]{3,2,1,0:T(8,128)S(1)}, u32[]{:S(2)}, u32[]{:S(2)}) collective-permute-start(f32[4,16,32,128]{3,2,1,0:T(8,128)} %param.2), channel_id=1, source_target_pairs={{0,8},{8,16},{16,24},{24,0},{1,9},{9,17},{17,25},{25,1},{2,10},{10... | collective-permute-start | bytes 3145736 | tf_op jit(solution)/shard_map/ppermute | solution.py:20
  9.5 47.0 %collective-permute-start = (f32[4,16,32,128]{3,2,1,0:T(8,128)}, f32[4,16,32,128]{3,2,1,0:T(8,128)S(1)}, u32[]{:S(2)}, u32[]{:S(2)}) collective-permute-start(f32[4,16,32,128]{3,2,1,0:T(8,128)} %param.2), channel_id=1, source_target_pairs={{8,0},{16,8},{24,16},{0,24},{9,1},{17,9},{25,17},{1,25},{10,2},{18... | collective-permute-start | bytes 3145736 | tf_op jit(solution)/shard_map/ppermute | solution.py:21
  16.4 4.3 copy-start.12
  69.5 26.0 %collective-permute-start.2 = (f32[4,16,32,128]{3,2,1,0:T(8,128)S(1)}, f32[4,16,32,128]{3,2,1,0:T(8,128)S(1)}, u32[]{:S(2)}, u32[]{:S(2)}) collective-permute-start(f32[4,16,32,128]{3,2,1,0:T(8,128)S(1)} %get-tuple-element.23), channel_id=1, source_target_pairs={{8,0},{16,8},{24,16},{0,24},{9,1},{17,9},{25,17},{1,25},{10,2},{18... | collective-permute-start | bytes 3145736 | tf_op jit(solution)/shard_map/ppermute | solution.py:21
  71.0 45.2 %collective-permute-start.3 = (f32[4,16,32,128]{3,2,1,0:T(8,128)S(1)}, f32[4,16,32,128]{3,2,1,0:T(8,128)S(1)}, u32[]{:S(2)}, u32[]{:S(2)}) collective-permute-start(f32[4,16,32,128]{3,2,1,0:T(8,128)S(1)} %get-tuple-element.23), channel_id=1, source_target_pairs={{0,8},{8,16},{16,24},{24,0},{1,9},{9,17},{17,25},{25,1},{2,10},{10... | collective-permute-start | bytes 3145736 | tf_op jit(solution)/shard_map/ppermute | solution.py:20
  95.6 20.6 %copy-start.10 = (f32[4,16,32,128]{3,2,1,0:T(8,128)}, f32[4,16,32,128]{3,2,1,0:T(8,128)S(1)}, u32[]{:S(2)}) copy-start(f32[4,16,32,128]{3,2,1,0:T(8,128)S(1)} %collective-permute-done.2) | copy-start | bytes 3145732
  116.2 1.0 copy-start.11
  126.0 26.0 %collective-permute-start.4 = (f32[4,16,32,128]{3,2,1,0:T(8,128)S(1)}, f32[4,16,32,128]{3,2,1,0:T(8,128)S(1)}, u32[]{:S(2)}, u32[]{:S(2)}) collective-permute-start(f32[4,16,32,128]{3,2,1,0:T(8,128)S(1)} %multiply_subtract_fusion.2), channel_id=1, source_target_pairs={{8,0},{16,8},{24,16},{0,24},{9,1},{17,9},{25,17},{1,25},{10,2},{18... | collective-permute-start | bytes 3145736 | tf_op jit(solution)/shard_map/ppermute | solution.py:21
  128.3 44.2 %collective-permute-start.5 = (f32[4,16,32,128]{3,2,1,0:T(8,128)S(1)}, f32[4,16,32,128]{3,2,1,0:T(8,128)S(1)}, u32[]{:S(2)}, u32[]{:S(2)}) collective-permute-start(f32[4,16,32,128]{3,2,1,0:T(8,128)S(1)} %multiply_subtract_fusion.2), channel_id=1, source_target_pairs={{0,8},{8,16},{16,24},{24,0},{1,9},{9,17},{17,25},{25,1},{2,10},{10... | collective-permute-start | bytes 3145736 | tf_op jit(solution)/shard_map/ppermute | solution.py:20
  152.1 20.4 %copy-start.7 = (f32[4,16,32,128]{3,2,1,0:T(8,128)}, f32[4,16,32,128]{3,2,1,0:T(8,128)S(1)}, u32[]{:S(2)}) copy-start(f32[4,16,32,128]{3,2,1,0:T(8,128)S(1)} %collective-permute-done.4) | copy-start | bytes 3145732
  172.5 1.0 copy-start.9
  182.6 26.0 %collective-permute-start.6 = (f32[4,16,32,128]{3,2,1,0:T(8,128)S(1)}, f32[4,16,32,128]{3,2,1,0:T(8,128)S(1)}, u32[]{:S(2)}, u32[]{:S(2)}) collective-permute-start(f32[4,16,32,128]{3,2,1,0:T(8,128)S(1)} %multiply_subtract_fusion.1), channel_id=1, source_target_pairs={{8,0},{16,8},{24,16},{0,24},{9,1},{17,9},{25,17},{1,25},{10,2},{18... | collective-permute-start | bytes 3145736 | tf_op jit(solution)/shard_map/ppermute | solution.py:21
  184.1 44.0 %collective-permute-start.7 = (f32[4,16,32,128]{3,2,1,0:T(8,128)S(1)}, f32[4,16,32,128]{3,2,1,0:T(8,128)S(1)}, u32[]{:S(2)}, u32[]{:S(2)}) collective-permute-start(f32[4,16,32,128]{3,2,1,0:T(8,128)S(1)} %multiply_subtract_fusion.1), channel_id=1, source_target_pairs={{0,8},{8,16},{16,24},{24,0},{1,9},{9,17},{17,25},{25,1},{2,10},{10... | collective-permute-start | bytes 3145736 | tf_op jit(solution)/shard_map/ppermute | solution.py:20
  190.2 38.9 %copy-start.13 = (f32[4,16,32]{2,1,0:T(8,128)S(1)}, f32[4,16,32]{2,1,0:T(8,128)}, u32[]{:S(2)}) copy-start(f32[4,16,32]{2,1,0:T(8,128)} %param.3) | copy-start | bytes 24580
  208.7 19.4 %copy-start.6 = (f32[4,16,32,128]{3,2,1,0:T(8,128)}, f32[4,16,32,128]{3,2,1,0:T(8,128)S(1)}, u32[]{:S(2)}) copy-start(f32[4,16,32,128]{3,2,1,0:T(8,128)S(1)} %collective-permute-done.6) | copy-start | bytes 3145732
  228.1 1.0 copy-start.8
  237.4 116.6 %all-reduce.4.cloned.1.call-start = ((), (), s32[]{:S(2)}) async-start(), calls=%async_computation.1 | async-start | bytes 2359296 | tf_op jit(solution)/shard_map/psum | solution.py:64
  285.0 10.7 %copy-start.1 = (f32[2048,512]{0,1:T(8,128)S(1)}, f32[2048,512]{0,1:T(8,128)}, u32[]{:S(2)}) copy-start(f32[2048,512]{0,1:T(8,128)} %all-gather.2.cloned.1.call-done) | copy-start | bytes 12582916
  354.0 1.8 copy-start.3
  413.1 82.3 %copy-start.4 = (f32[512,512]{1,0:T(8,128)S(1)}, f32[512,512]{1,0:T(8,128)}, u32[]{:S(2)}) copy-start(f32[512,512]{1,0:T(8,128)} %fusion.125) | copy-start | bytes 3145732
  497.1 1.2 copy-start.14
  498.2 2.2 copy-start.2
  500.4 2.9 copy-start.5
Sparse Core Ops, SparseCore 0:
  237.5 47.3 all-gather.1
  300.8 53.1 all-reduce.3
where the time goes:
time: 522 us; the launch traced here: 515 us
  waiting for transfers between devices  252 us (48%)
  other arithmetic  152 us (29%)
  local copies, waits for them, and re-layouts  54.5 us (10%)
  matrix products  29 us (6%)
  between operations  17 us (3%)
  starting transfers between devices  10.5 us (2%)
    another operation x14, other arithmetic, per_device(): lower_factor = jnp.linalg.cholesky(gram_full)  82.5 us
    ppermute x4, waiting for transfers between devices, padded_2(): after = lax.ppermute(leading, axis, down)  79.4 us
    ppermute x4, waiting for transfers between devices, padded_2(): before = lax.ppermute(last, axis, up)  74 us
    psum x1, waiting for transfers between devices, per_device(): gram_full, coupling = lax.psum((gram_part, coupling_part), 'space')  51 us
    all_gather x1, waiting for transfers between devices, per_device(): panel = lax.all_gather(panel_own, 'orb', axis=1, tiled=True)  47.5 us
    another operation x4, other arithmetic, per_device(): lax.linalg.triangular_solve(lower_factor, identity, left_side=True, lower...  40.3 us
    slice x64, local copies, waits for them, and re-layouts, hamilton(): jnp.roll(field, offset, axis) + jnp.roll(field, -offset, axis)  35.9 us
    sub x3, other arithmetic, chebyshev(): 2.0 * (hamilton(current, potential) - SHIFT_MID * current) / HALF_WIDTH  20.7 us
  transfers between devices with their start and end apart: 10, of which 10 were waited for; matrix products, arithmetic and copies ran while one was open for 5% of the time, Pallas kernels for 0%

commit v1 on v0

--- a/solution.py
+++ b/solution.py
@@ -8,6 +8,18 @@
 STENCIL = (-205.0 / 72.0, 8.0 / 5.0, -1.0 / 5.0, 8.0 / 315.0, -1.0 / 560.0)
 SHIFT_MID = 7.25
 HALF_WIDTH = 4.75
+
+
+def ring_gather(array, axis, dim):
+    ways, here, lap = (lax.axis_size(axis), lax.axis_index(axis), array.shape[dim])
+    shape = [n * ways if d == dim else n for d, n in enumerate(array.shape)]
+    full = lax.dynamic_update_slice_in_dim(
+        jnp.zeros(shape, array.dtype), array, here * lap, axis=dim
+    )
+    for far in range(1, ways):
+        array = lax.ppermute(array, axis, [(d, (d + 1) % ways) for d in range(ways)])
+        full = lax.dynamic_update_slice_in_dim(full, array, (here - far) % ways * lap, axis=dim)
+    return full
 
 
 def padded_2(shard, sides, width):
@@ -58,7 +70,7 @@
     flat = filtered.reshape(local_points, columns)
     panel_own = flat[:, :panel_dev]
     trailing = flat[:, panel_dev:]
-    panel = lax.all_gather(panel_own, "orb", axis=1, tiled=True)
+    panel = ring_gather(panel_own, "orb", 1)
     coupling_part = jnp.dot(panel.T, trailing, precision=highest)
     gram_part = jnp.dot(panel.T, panel, precision=highest)
     gram_full, coupling = lax.psum((gram_part, coupling_part), "space")

time: 522 us -> 607 us (1.16)
  local copies, waits for them, and re-layouts: 54.5 us -> 119 us
  waiting for transfers between devices: 252 us -> 268 us
    ppermute x0 -> x7, waiting for transfers between devices: none -> 62.7 us  [ring_gather(): lax.ppermute(array, axis, [(d, (d + 1) % ways) for d in range(ways)])]
    dynamic_update_slice x0 -> x8, local copies, waits for them, and re-layouts: none -> 48.5 us  [the longest x7 42.6 us: ring_gather(): lax.dynamic_update_slice_in_dim(full, array, (here - far) % ways * lap, a...]
    all_gather x1 -> x0, waiting for transfers between devices: 47.5 us -> none  [per_device(): panel = lax.all_gather(panel_own, 'orb', axis=1, tiled=True)]
    ppermute x0 -> x7, local copies, waits for them, and re-layouts: none -> 9.58 us  [ring_gather(): lax.ppermute(array, axis, [(d, (d + 1) % ways) for d in range(ways)])]
  transfers between devices with their start and end apart: 10 -> 16, of which waited for: 10 -> 15; matrix products, arithmetic and copies ran while one was open for 5% -> 13% of each run, Pallas kernels for 0% -> 0%
where the time goes in v1:
time: 607 us; the launch traced here: 598 us
  waiting for transfers between devices  268 us (44%)
  other arithmetic  152 us (25%)
  local copies, waits for them, and re-layouts  119 us (20%)
  matrix products  30.9 us (5%)
  between operations  16.8 us (3%)
  starting transfers between devices  10.9 us (2%)
    another operation x14, other arithmetic, per_device(): lower_factor = jnp.linalg.cholesky(gram_full)  82.6 us
    ppermute x4, waiting for transfers between devices, padded_2(): after = lax.ppermute(leading, axis, down)  79.1 us
    ppermute x4, waiting for transfers between devices, padded_2(): before = lax.ppermute(last, axis, up)  74 us
    ppermute x7, waiting for transfers between devices, ring_gather(): lax.ppermute(array, axis, [(d, (d + 1) % ways) for d in range(ways)])  62.7 us
    psum x1, waiting for transfers between devices, per_device(): gram_full, coupling = lax.psum((gram_part, coupling_part), 'space')  52.6 us
    dynamic_update_slice x7, local copies, waits for them, and re-layouts, ring_gather(): lax.dynamic_update_slice_in_dim(full, array, (here - far) % ways * lap, a...  42.6 us
    another operation x4, other arithmetic, per_device(): lax.linalg.triangular_solve(lower_factor, identity, left_side=True, lower...  40.3 us
    slice x64, local copies, waits for them, and re-layouts, hamilton(): jnp.roll(field, offset, axis) + jnp.roll(field, -offset, axis)  36 us
  transfers between devices with their start and end apart: 16, of which 15 were waited for; matrix products, arithmetic and copies ran while one was open for 13% of the time, Pallas kernels for 0%

profile of v1, /device:TPU:0, one launch (start us, length us, event | category | flops | bytes accessed | tf_op | source)
XLA Modules:
  0.0 598.1 jit_solution(16869442312271368046)
XLA Ops:
  6.5 3.0 collective-permute-start.1
  10.5 1.9 fusion.217
  21.2 13.6 %collective-permute-done.1 = f32[4,16,32,128]{3,2,1,0:T(8,128)S(1)} collective-permute-done((f32[4,16,32,128]{3,2,1,0:T(8,128)}, f32[4,16,32,128]{3,2,1,0:T(8,128)S(1)}, u32[]{:S(2)}, u32[]{:S(2)}) %collective-permute-start.1) | collective-permute-done | bytes 1048608 | tf_op jit(solution)/shard_map/ppermute | solution.py:32
  35.0 21.6 %collective-permute-done = f32[4,16,32,128]{3,2,1,0:T(8,128)S(1)} collective-permute-done((f32[4,16,32,128]{3,2,1,0:T(8,128)}, f32[4,16,32,128]{3,2,1,0:T(8,128)S(1)}, u32[]{:S(2)}, u32[]{:S(2)}) %collective-permute-start) | collective-permute-done | bytes 1048608 | tf_op jit(solution)/shard_map/ppermute | solution.py:33
  56.6 5.3 broadcast_multiply_fusion.1
  73.0 22.7 %collective-permute-done.2 = f32[4,16,32,128]{3,2,1,0:T(8,128)S(1)} collective-permute-done((f32[4,16,32,128]{3,2,1,0:T(8,128)S(1)}, f32[4,16,32,128]{3,2,1,0:T(8,128)S(1)}, u32[]{:S(2)}, u32[]{:S(2)}) %collective-permute-start.2) | collective-permute-done | bytes 1048608 | tf_op jit(solution)/shard_map/ppermute | solution.py:33
  95.6 20.6 %collective-permute-done.3 = f32[4,16,32,128]{3,2,1,0:T(8,128)S(1)} collective-permute-done((f32[4,16,32,128]{3,2,1,0:T(8,128)S(1)}, f32[4,16,32,128]{3,2,1,0:T(8,128)S(1)}, u32[]{:S(2)}, u32[]{:S(2)}) %collective-permute-start.3) | collective-permute-done | bytes 1048608 | tf_op jit(solution)/shard_map/ppermute | solution.py:32
  117.2 6.9 %multiply_subtract_fusion.2 = f32[4,16,32,128]{3,2,1,0:T(8,128)S(1)} fusion(f32[4,16,32,128]{3,2,1,0:T(8,128)S(1)} %copy-done, f32[4,16,32,128]{3,2,1,0:T(8,128)S(1)} %get-tuple-element.24, f32[4,16,4,128]{3,2,1,0:T(4,128)} %get-tuple-element.122, f32[4,16,28,128]{3,2,1,0:T(8,128)S(1)} %get-tuple-element.124, f32[4,16,28,128]{3,2,1,0:T(8,128)S(1)} %get-tuple-element.123, ...), kind=kLoop, calls=%fused_computation.201 | loop fusion | flops 17301504 | bytes 23076864 | tf_op jit(solution)/shard_map/sub | solution.py:58
  126.1 2.3 collective-permute-start.4
  135.5 16.7 %collective-permute-done.4 = f32[4,16,32,128]{3,2,1,0:T(8,128)S(1)} collective-permute-done((f32[4,16,32,128]{3,2,1,0:T(8,128)S(1)}, f32[4,16,32,128]{3,2,1,0:T(8,128)S(1)}, u32[]{:S(2)}, u32[]{:S(2)}) %collective-permute-start.4) | collective-permute-done | bytes 1048608 | tf_op jit(solution)/shard_map/ppermute | solution.py:33
  152.1 20.4 %collective-permute-done.5 = f32[4,16,32,128]{3,2,1,0:T(8,128)S(1)} collective-permute-done((f32[4,16,32,128]{3,2,1,0:T(8,128)S(1)}, f32[4,16,32,128]{3,2,1,0:T(8,128)S(1)}, u32[]{:S(2)}, u32[]{:S(2)}) %collective-permute-start.5) | collective-permute-done | bytes 1048608 | tf_op jit(solution)/shard_map/ppermute | solution.py:32
  173.5 7.0 %multiply_subtract_fusion.1 = f32[4,16,32,128]{3,2,1,0:T(8,128)S(1)} fusion(f32[4,16,32,128]{3,2,1,0:T(8,128)S(1)} %multiply_subtract_fusion.2, f32[4,16,4,128]{3,2,1,0:T(4,128)} %get-tuple-element.90, f32[4,16,28,128]{3,2,1,0:T(8,128)S(1)} %get-tuple-element.92, f32[4,16,28,128]{3,2,1,0:T(8,128)S(1)} %get-tuple-element.91, ...), kind=kLoop, calls=%fused_computation.200 | loop fusion | flops 17563648 | bytes 22028288 | tf_op jit(solution)/shard_map/sub | solution.py:58
  190.6 18.2 %collective-permute-done.6 = f32[4,16,32,128]{3,2,1,0:T(8,128)S(1)} collective-permute-done((f32[4,16,32,128]{3,2,1,0:T(8,128)S(1)}, f32[4,16,32,128]{3,2,1,0:T(8,128)S(1)}, u32[]{:S(2)}, u32[]{:S(2)}) %collective-permute-start.6) | collective-permute-done | bytes 1048608 | tf_op jit(solution)/shard_map/ppermute | solution.py:33
  208.8 19.4 %collective-permute-done.7 = f32[4,16,32,128]{3,2,1,0:T(8,128)S(1)} collective-permute-done((f32[4,16,32,128]{3,2,1,0:T(8,128)S(1)}, f32[4,16,32,128]{3,2,1,0:T(8,128)S(1)}, u32[]{:S(2)}, u32[]{:S(2)}) %collective-permute-start.7) | collective-permute-done | bytes 1048608 | tf_op jit(solution)/shard_map/ppermute | solution.py:32
  229.2 7.0 %multiply_subtract_fusion = f32[4,16,32,128]{3,2,1,0:T(8,128)S(1)} fusion(f32[4,16,32,128]{3,2,1,0:T(8,128)S(1)} %multiply_subtract_fusion.2, f32[4,16,32,128]{3,2,1,0:T(8,128)S(1)} %multiply_subtract_fusion.1, f32[4,16,4,128]{3,2,1,0:T(4,128)} %get-tuple-element.58, f32[4,16,28,128]{3,2,1,0:T(8,128)S(1)} %get-tuple-element.60, ...), kind=kLoop, calls=%fused_computation.199 | loop fusion | flops 17301504 | bytes 22028288 | tf_op jit(solution)/shard_map/sub | solution.py:58
  237.7 10.6 %collective-permute-done.8 = f32[2048,64]{0,1:T(8,128)S(1)} collective-permute-done((f32[2048,64]{0,1:T(8,128)}, f32[2048,64]{0,1:T(8,128)S(1)}, u32[]{:S(2)}, u32[]{:S(2)}) %collective-permute-start.8) | collective-permute-done | bytes 524320 | tf_op jit(solution)/shard_map/ppermute | solution.py:20
  249.1 10.4 %collective-permute-done.9 = f32[2048,64]{0,1:T(8,128)S(1)} collective-permute-done((f32[2048,64]{0,1:T(8,128)S(1)}, f32[2048,64]{0,1:T(8,128)S(1)}, u32[]{:S(2)}, u32[]{:S(2)}) %collective-permute-start.9) | collective-permute-done | bytes 524320 | tf_op jit(solution)/shard_map/ppermute | solution.py:20
  260.3 10.4 %collective-permute-done.10 = f32[2048,64]{0,1:T(8,128)S(1)} collective-permute-done((f32[2048,64]{0,1:T(8,128)S(1)}, f32[2048,64]{0,1:T(8,128)S(1)}, u32[]{:S(2)}, u32[]{:S(2)}) %collective-permute-start.10) | collective-permute-done | bytes 524320 | tf_op jit(solution)/shard_map/ppermute | solution.py:20
  271.5 10.4 %collective-permute-done.11 = f32[2048,64]{0,1:T(8,128)S(1)} collective-permute-done((f32[2048,64]{0,1:T(8,128)S(1)}, f32[2048,64]{0,1:T(8,128)S(1)}, u32[]{:S(2)}, u32[]{:S(2)}) %collective-permute-start.11) | collective-permute-done | bytes 524320 | tf_op jit(solution)/shard_map/ppermute | solution.py:20
  282.7 10.4 %collective-permute-done.12 = f32[2048,64]{0,1:T(8,128)S(1)} collective-permute-done((f32[2048,64]{0,1:T(8,128)S(1)}, f32[2048,64]{0,1:T(8,128)S(1)}, u32[]{:S(2)}, u32[]{:S(2)}) %collective-permute-start.12) | collective-permute-done | bytes 524320 | tf_op jit(solution)/shard_map/ppermute | solution.py:20
  293.9 10.5 %collective-permute-done.13 = f32[2048,64]{0,1:T(8,128)} collective-permute-done((f32[2048,64]{0,1:T(8,128)S(1)}, f32[2048,64]{0,1:T(8,128)}, u32[]{:S(2)}, u32[]{:S(2)}) %collective-permute-start.13) | collective-permute-done | bytes 524320 | tf_op jit(solution)/shard_map/ppermute | solution.py:20
  304.7 2.6 broadcast_in_dim.3
  307.3 5.9 dynamic_update_slice.24
  314.6 5.9 dynamic_update_slice.25
  321.9 5.1 dynamic_update_slice.26
  328.4 6.6 %dynamic_update_slice.27 = f32[2048,512]{1,0:T(8,128)} dynamic-update-slice(f32[2048,512]{1,0:T(8,128)} %dynamic_update_slice.26, f32[2048,64]{1,0:T(8,128)S(1)} %copy.14, s32[]{:T(128)} %copy.52, s32[]{:T(128)S(6)} %select_n.66) | dynamic-update-slice | bytes 1048580 | tf_op jit(solution)/shard_map/dynamic_update_slice | solution.py:21
  336.4 5.9 dynamic_update_slice.28
  343.6 6.6 %dynamic_update_slice.29 = f32[2048,512]{1,0:T(8,128)} dynamic-update-slice(f32[2048,512]{1,0:T(8,128)} %dynamic_update_slice.28, f32[2048,64]{1,0:T(8,128)S(1)} %copy.16, s32[]{:T(128)} %copy.52, s32[]{:T(128)S(6)} %select_n.70) | dynamic-update-slice | bytes 1048580 | tf_op jit(solution)/shard_map/dynamic_update_slice | solution.py:21
  351.6 5.9 dynamic_update_slice.30
  358.8 6.6 %dynamic_update_slice.31 = f32[2048,512]{1,0:T(8,128)} dynamic-update-slice(f32[2048,512]{1,0:T(8,128)} %dynamic_update_slice.30, f32[2048,64]{1,0:T(8,128)S(1)} %copy.18, s32[]{:T(128)} %copy.52, s32[]{:T(128)S(6)} %select_n.74) | dynamic-update-slice | bytes 1048580 | tf_op jit(solution)/shard_map/dynamic_update_slice | solution.py:21
  365.5 11.5 %fusion.224 = f32[512,512]{0,1:T(8,128)} fusion(f32[2048,512]{1,0:T(8,128)} %dynamic_update_slice.31), kind=kOutput, calls=%fused_computation.337 | convolution fusion | flops 6442450944 | bytes 5242880 | tf_op jit(solution)/shard_map/dot_general | solution.py:75
  377.0 3.4 fusion.154
  382.7 52.6 %all-reduce.4.cloned.1.call-done = (f32[512,64]{0,1:T(8,128)}, f32[512,512]{0,1:T(8,128)}) async-done(((f32[512,64]{0,1:T(8,128)}, f32[512,512]{0,1:T(8,128)}), (f32[512,64]{0,1:T(8,128)}, f32[512,512]{0,1:T(8,128)})) %all-reduce.4.cloned.1.call-update) | async-done | bytes 1179664 | tf_op jit(solution)/shard_map/psum | solution.py:76
  437.3 11.7 %cholesky.104 = f32[128,128]{1,0:T(8,128)S(1)} custom-call(f32[128,128]{1,0:T(8,128)S(1)} %cholesky.266), custom_call_target="Cholesky" | custom-call | tf_op jit(solution)/shard_map/jit(cholesky)/cholesky | solution.py:79
  449.1 9.8 %custom-call.30 = f32[1,128,128]{1,2,0:T(8,128)S(1)} custom-call(f32[1,128,128]{2,1,0:T(8,128)S(1)} %get-tuple-element.168), custom_call_target="InvertDiagBlocksLowerTriangular" | custom-call | tf_op jit(solution)/shard_map/jit(cholesky)/cholesky | solution.py:79
  459.6 12.2 %cholesky.217 = f32[128,128]{1,0:T(8,128)S(1)} custom-call(f32[128,128]{1,0:T(8,128)S(1)} %cholesky.270), custom_call_target="Cholesky" | custom-call | tf_op jit(solution)/shard_map/jit(cholesky)/cholesky | solution.py:79
  471.8 9.8 %custom-call.31 = f32[1,128,128]{1,2,0:T(8,128)S(1)} custom-call(f32[1,128,128]{2,1,0:T(8,128)S(1)} %get-tuple-element.165), custom_call_target="InvertDiagBlocksLowerTriangular" | custom-call | tf_op jit(solution)/shard_map/jit(cholesky)/cholesky | solution.py:79
  482.3 12.3 %cholesky.238 = f32[128,128]{1,0:T(8,128)} custom-call(f32[128,128]{1,0:T(8,128)S(1)} %cholesky.275), custom_call_target="Cholesky" | custom-call | tf_op jit(solution)/shard_map/jit(cholesky)/cholesky | solution.py:79
  496.8 11.3 %custom-call.32 = f32[1,128,128]{1,2,0:T(8,128)} custom-call(f32[1,128,128]{2,1,0:T(8,128)} %get-tuple-element.162), custom_call_target="InvertDiagBlocksLowerTriangular" | custom-call | tf_op jit(solution)/shard_map/jit(cholesky)/cholesky | solution.py:79
  509.6 11.9 %cholesky.255 = f32[128,128]{1,0:T(8,128)S(1)} custom-call(f32[128,128]{1,0:T(8,128)S(1)} %convolution_subtract_fusion.6), custom_call_target="Cholesky" | custom-call | tf_op jit(solution)/shard_map/jit(cholesky)/cholesky | solution.py:79
  525.3 10.2 %while.1 = (s32[]{:T(128)}, f32[512,512]{1,0:T(8,128)S(1)}, s32[4,2]{0,1:T(2,128)S(1)}, f32[4,128,128]{2,1,0:T(8,128)}, s32[]{:T(128)}) while((s32[]{:T(128)}, f32[512,512]{1,0:T(8,128)S(1)}, s32[4,2]{0,1:T(2,128)S(1)}, f32[4,128,128]{2,1,0:T(8,128)}, s32[]{:T(128)}) %tuple.94), condition=%wide.while_cond, body=%wide.while_body.sunk | while | flops 2 | bytes 132705 | solution.py:81
  525.9 2.0 bitcast_dynamic-update-slice_fusion.2
  528.4 1.9 bitcast_dynamic-update-slice_fusion.2
  531.0 1.9 bitcast_dynamic-update-slice_fusion.2
  533.5 1.9 bitcast_dynamic-update-slice_fusion.2
  535.5 40.1 %custom-call.33 = f32[4,128,128]{1,2,0:T(8,128)S(1)} custom-call(f32[4,128,128]{2,1,0:T(8,128)} %get-tuple-element.12), custom_call_target="InvertDiagBlocksLowerTriangular" | custom-call | tf_op jit(solution)/shard_map/triangular_solve | solution.py:81
  579.3 4.2 fusion.138
  585.5 4.2 convolution_subtract_fusion
  (179 shorter events, 78.3 us)
Async XLA Ops:
  6.5 5.8 copy-start
  6.5 428.7 %all-reduce.4.cloned.1.call-start = ((), (), s32[]{:S(2)}) async-start(), calls=%async_computation | async-start | bytes 2359296 | tf_op jit(solution)/shard_map/psum | solution.py:76
  6.5 28.2 %collective-permute-start.1 = (f32[4,16,32,128]{3,2,1,0:T(8,128)}, f32[4,16,32,128]{3,2,1,0:T(8,128)S(1)}, u32[]{:S(2)}, u32[]{:S(2)}) collective-permute-start(f32[4,16,32,128]{3,2,1,0:T(8,128)} %param.2), channel_id=1, source_target_pairs={{0,8},{8,16},{16,24},{24,0},{1,9},{9,17},{17,25},{25,1},{2,10},{10... | collective-permute-start | bytes 3145736 | tf_op jit(solution)/shard_map/ppermute | solution.py:32
  9.5 47.0 %collective-permute-start = (f32[4,16,32,128]{3,2,1,0:T(8,128)}, f32[4,16,32,128]{3,2,1,0:T(8,128)S(1)}, u32[]{:S(2)}, u32[]{:S(2)}) collective-permute-start(f32[4,16,32,128]{3,2,1,0:T(8,128)} %param.2), channel_id=1, source_target_pairs={{8,0},{16,8},{24,16},{0,24},{9,1},{17,9},{25,17},{1,25},{10,2},{18... | collective-permute-start | bytes 3145736 | tf_op jit(solution)/shard_map/ppermute | solution.py:33
  16.4 4.3 copy-start.17
  69.6 26.0 %collective-permute-start.2 = (f32[4,16,32,128]{3,2,1,0:T(8,128)S(1)}, f32[4,16,32,128]{3,2,1,0:T(8,128)S(1)}, u32[]{:S(2)}, u32[]{:S(2)}) collective-permute-start(f32[4,16,32,128]{3,2,1,0:T(8,128)S(1)} %get-tuple-element.23), channel_id=1, source_target_pairs={{8,0},{16,8},{24,16},{0,24},{9,1},{17,9},{25,17},{1,25},{10,2},{18... | collective-permute-start | bytes 3145736 | tf_op jit(solution)/shard_map/ppermute | solution.py:33
  71.0 45.2 %collective-permute-start.3 = (f32[4,16,32,128]{3,2,1,0:T(8,128)S(1)}, f32[4,16,32,128]{3,2,1,0:T(8,128)S(1)}, u32[]{:S(2)}, u32[]{:S(2)}) collective-permute-start(f32[4,16,32,128]{3,2,1,0:T(8,128)S(1)} %get-tuple-element.23), channel_id=1, source_target_pairs={{0,8},{8,16},{16,24},{24,0},{1,9},{9,17},{17,25},{25,1},{2,10},{10... | collective-permute-start | bytes 3145736 | tf_op jit(solution)/shard_map/ppermute | solution.py:32
  95.6 20.6 %copy-start.10 = (f32[4,16,32,128]{3,2,1,0:T(8,128)}, f32[4,16,32,128]{3,2,1,0:T(8,128)S(1)}, u32[]{:S(2)}) copy-start(f32[4,16,32,128]{3,2,1,0:T(8,128)S(1)} %collective-permute-done.2) | copy-start | bytes 3145732
  116.2 1.0 copy-start.11
  126.1 26.0 %collective-permute-start.4 = (f32[4,16,32,128]{3,2,1,0:T(8,128)S(1)}, f32[4,16,32,128]{3,2,1,0:T(8,128)S(1)}, u32[]{:S(2)}, u32[]{:S(2)}) collective-permute-start(f32[4,16,32,128]{3,2,1,0:T(8,128)S(1)} %multiply_subtract_fusion.2), channel_id=1, source_target_pairs={{8,0},{16,8},{24,16},{0,24},{9,1},{17,9},{25,17},{1,25},{10,2},{18... | collective-permute-start | bytes 3145736 | tf_op jit(solution)/shard_map/ppermute | solution.py:33
  128.4 44.2 %collective-permute-start.5 = (f32[4,16,32,128]{3,2,1,0:T(8,128)S(1)}, f32[4,16,32,128]{3,2,1,0:T(8,128)S(1)}, u32[]{:S(2)}, u32[]{:S(2)}) collective-permute-start(f32[4,16,32,128]{3,2,1,0:T(8,128)S(1)} %multiply_subtract_fusion.2), channel_id=1, source_target_pairs={{0,8},{8,16},{16,24},{24,0},{1,9},{9,17},{17,25},{25,1},{2,10},{10... | collective-permute-start | bytes 3145736 | tf_op jit(solution)/shard_map/ppermute | solution.py:32
  152.1 20.4 %copy-start.7 = (f32[4,16,32,128]{3,2,1,0:T(8,128)}, f32[4,16,32,128]{3,2,1,0:T(8,128)S(1)}, u32[]{:S(2)}) copy-start(f32[4,16,32,128]{3,2,1,0:T(8,128)S(1)} %collective-permute-done.4) | copy-start | bytes 3145732
  172.6 1.0 copy-start.9
  182.8 26.0 %collective-permute-start.6 = (f32[4,16,32,128]{3,2,1,0:T(8,128)S(1)}, f32[4,16,32,128]{3,2,1,0:T(8,128)S(1)}, u32[]{:S(2)}, u32[]{:S(2)}) collective-permute-start(f32[4,16,32,128]{3,2,1,0:T(8,128)S(1)} %multiply_subtract_fusion.1), channel_id=1, source_target_pairs={{8,0},{16,8},{24,16},{0,24},{9,1},{17,9},{25,17},{1,25},{10,2},{18... | collective-permute-start | bytes 3145736 | tf_op jit(solution)/shard_map/ppermute | solution.py:33
  184.2 44.0 %collective-permute-start.7 = (f32[4,16,32,128]{3,2,1,0:T(8,128)S(1)}, f32[4,16,32,128]{3,2,1,0:T(8,128)S(1)}, u32[]{:S(2)}, u32[]{:S(2)}) collective-permute-start(f32[4,16,32,128]{3,2,1,0:T(8,128)S(1)} %multiply_subtract_fusion.1), channel_id=1, source_target_pairs={{0,8},{8,16},{16,24},{24,0},{1,9},{9,17},{17,25},{25,1},{2,10},{10... | collective-permute-start | bytes 3145736 | tf_op jit(solution)/shard_map/ppermute | solution.py:32
  190.4 38.8 %copy-start.18 = (f32[4,16,32]{2,1,0:T(8,128)S(1)}, f32[4,16,32]{2,1,0:T(8,128)}, u32[]{:S(2)}) copy-start(f32[4,16,32]{2,1,0:T(8,128)} %param.3) | copy-start | bytes 24580
  208.8 19.4 %copy-start.6 = (f32[4,16,32,128]{3,2,1,0:T(8,128)}, f32[4,16,32,128]{3,2,1,0:T(8,128)S(1)}, u32[]{:S(2)}) copy-start(f32[4,16,32,128]{3,2,1,0:T(8,128)S(1)} %collective-permute-done.6) | copy-start | bytes 3145732
  228.3 1.0 copy-start.8
  237.7 10.6 %collective-permute-start.8 = (f32[2048,64]{0,1:T(8,128)}, f32[2048,64]{0,1:T(8,128)S(1)}, u32[]{:S(2)}, u32[]{:S(2)}) collective-permute-start(f32[2048,64]{0,1:T(8,128)} %copy.11), channel_id=1, source_target_pairs={{0,1},{1,2},{2,3},{3,4},{4,5},{5,6},{6,7},{7,0},{8,9},{9,10},{10,1... | collective-permute-start | bytes 1572872 | tf_op jit(solution)/shard_map/ppermute | solution.py:20
  248.3 0.8 copy-start.12
  249.1 10.4 %collective-permute-start.9 = (f32[2048,64]{0,1:T(8,128)S(1)}, f32[2048,64]{0,1:T(8,128)S(1)}, u32[]{:S(2)}, u32[]{:S(2)}) collective-permute-start(f32[2048,64]{0,1:T(8,128)S(1)} %collective-permute-done.8), channel_id=1, source_target_pairs={{0,1},{1,2},{2,3},{3,4},{4,5},{5,6},{6,7},{7,0},{8,9},{9,10},{10,1... | collective-permute-start | bytes 1572872 | tf_op jit(solution)/shard_map/ppermute | solution.py:20
  259.5 0.8 copy-start.13
  260.3 10.4 %collective-permute-start.10 = (f32[2048,64]{0,1:T(8,128)S(1)}, f32[2048,64]{0,1:T(8,128)S(1)}, u32[]{:S(2)}, u32[]{:S(2)}) collective-permute-start(f32[2048,64]{0,1:T(8,128)S(1)} %collective-permute-done.9), channel_id=1, source_target_pairs={{0,1},{1,2},{2,3},{3,4},{4,5},{5,6},{6,7},{7,0},{8,9},{9,10},{10,1... | collective-permute-start | bytes 1572872 | tf_op jit(solution)/shard_map/ppermute | solution.py:20
  270.7 0.8 copy-start.14
  271.5 10.4 %collective-permute-start.11 = (f32[2048,64]{0,1:T(8,128)S(1)}, f32[2048,64]{0,1:T(8,128)S(1)}, u32[]{:S(2)}, u32[]{:S(2)}) collective-permute-start(f32[2048,64]{0,1:T(8,128)S(1)} %collective-permute-done.10), channel_id=1, source_target_pairs={{0,1},{1,2},{2,3},{3,4},{4,5},{5,6},{6,7},{7,0},{8,9},{9,10},{10,1... | collective-permute-start | bytes 1572872 | tf_op jit(solution)/shard_map/ppermute | solution.py:20
  281.9 0.8 copy-start.15
  282.7 10.4 %collective-permute-start.12 = (f32[2048,64]{0,1:T(8,128)S(1)}, f32[2048,64]{0,1:T(8,128)S(1)}, u32[]{:S(2)}, u32[]{:S(2)}) collective-permute-start(f32[2048,64]{0,1:T(8,128)S(1)} %collective-permute-done.11), channel_id=1, source_target_pairs={{0,1},{1,2},{2,3},{3,4},{4,5},{5,6},{6,7},{7,0},{8,9},{9,10},{10,1... | collective-permute-start | bytes 1572872 | tf_op jit(solution)/shard_map/ppermute | solution.py:20
  293.1 0.8 copy-start.16
  293.9 10.5 %collective-permute-start.13 = (f32[2048,64]{0,1:T(8,128)S(1)}, f32[2048,64]{0,1:T(8,128)}, u32[]{:S(2)}, u32[]{:S(2)}) collective-permute-start(f32[2048,64]{0,1:T(8,128)S(1)} %collective-permute-done.12), channel_id=1, source_target_pairs={{0,1},{1,2},{2,3},{3,4},{4,5},{5,6},{6,7},{7,0},{8,9},{9,10},{10,1... | collective-permute-start | bytes 1572872 | tf_op jit(solution)/shard_map/ppermute | solution.py:20
  304.4 53.1 %collective-permute-start.14 = (f32[2048,64]{0,1:T(8,128)}, f32[2048,64]{0,1:T(8,128)}, u32[]{:S(2)}, u32[]{:S(2)}) collective-permute-start(f32[2048,64]{0,1:T(8,128)} %collective-permute-done.13), channel_id=1, source_target_pairs={{0,1},{1,2},{2,3},{3,4},{4,5},{5,6},{6,7},{7,0},{8,9},{9,10},{10,1... | collective-permute-start | bytes 1572872 | tf_op jit(solution)/shard_map/ppermute | solution.py:20
  365.5 11.5 %copy-start.1 = (f32[2048,512]{1,0:T(8,128)S(1)}, f32[2048,512]{1,0:T(8,128)}, u32[]{:S(2)}) copy-start(f32[2048,512]{1,0:T(8,128)} %dynamic_update_slice.31) | copy-start | bytes 12582916
  435.2 1.8 copy-start.3
  494.6 81.3 %copy-start.4 = (f32[512,512]{1,0:T(8,128)S(1)}, f32[512,512]{1,0:T(8,128)}, u32[]{:S(2)}) copy-start(f32[512,512]{1,0:T(8,128)} %fusion.125) | copy-start | bytes 3145732
  577.1 2.2 copy-start.2
  579.3 4.2 copy-start.19
  583.5 2.0 copy-start.5
Sparse Core Ops, SparseCore 0:
  380.5 54.7 all-reduce.3
